TPU v7x, 512 devices: a whole 4x8x8 slice. The times are simulated.
512 devices in a mesh: ctx: 64 (over y, z), tp: 8 (over x, core).
Axes of the slice: x: 4, y: 8, z: 8, core: 2. Of those that a mesh axis runs over, the one named last changes fastest.
Arguments:
- x_heads: bfloat16 [16384, 5120], P('ctx', 'tp'), may hold values from -6 to 6
- log_decay: float32 [80, 16384], P('tp', 'ctx'), may hold values from -1 to 0, as said below
- b_proj: bfloat16 [16384, 128], P('ctx'), may hold values from -6 to 6
- c_proj: bfloat16 [16384, 128], P('ctx'), may hold values from -6 to 6
- grad_out: bfloat16 [16384, 5120], P('ctx', 'tp'), may hold values from -0.00390625 to 0.00390625
Outputs:
- grad_x: bfloat16 [16384, 5120], P('ctx', 'tp')
- grad_b: float32 [16384, 128], P(('ctx', 'tp'))
- grad_c: float32 [16384, 128], P(('ctx', 'tp'))
Inputs may be any that keep to these rules, and one draw needn't show every extreme that they name: log_decay is negative everywhere.
All inputs are finite; a program needn't handle non-finite values.
Results may differ from a plain program's by a relative error of at most 0.0056.
Values sent between devices are 32-bit elements; how exact they have to be, the bound alone decides.
A program may use at most 128 MiB of HBM per device.

v0:
```python
import jax
import jax.numpy as jnp
from jax import lax
from jax.sharding import PartitionSpec as P

HEADDIM = 64
STATE = 128
GROUP = 256


def carried_in(x, axis, combine, identity, reverse):
    devices, here = (lax.axis_size(axis), lax.axis_index(axis))
    everything = jax.tree.map(lambda part: lax.all_gather(part, axis), x)
    start = jax.tree.map(
        lambda part, zero: jnp.broadcast_to(jnp.asarray(zero, part.dtype), part.shape), x, identity
    )

    def step(k, before):
        at = devices - 1 - k if reverse else k
        reached = at > here if reverse else at < here
        new = combine(before, jax.tree.map(lambda part: part[at], everything))
        return jax.tree.map(lambda a, b: jnp.where(reached, a, b), new, before)

    return lax.fori_loop(0, devices, step, start)


def link(earlier, later):
    return (earlier[0] * later[0], later[0][:, None, None] * earlier[1] + later[1])


def carry_forward(decays, state):
    start = (jnp.ones_like(decays), jnp.zeros_like(state))
    return carried_in((decays, state), "ctx", link, start, False)[1]


def carry_backward(decays, state):
    start = (jnp.ones_like(decays), jnp.zeros_like(state))
    return carried_in((decays, state), "ctx", link, start, True)[1]


def shards(x_heads, log_decay, b_proj, c_proj, grad_out):
    tokens = x_heads.shape[0]
    heads = log_decay.shape[0]
    nblock = tokens // GROUP
    xs = x_heads.reshape(nblock, GROUP, heads, HEADDIM)
    gs = grad_out.reshape(nblock, GROUP, heads, HEADDIM)
    bs = b_proj.reshape(nblock, GROUP, STATE)
    cs = c_proj.reshape(nblock, GROUP, STATE)
    cums = jnp.cumsum(log_decay.reshape(heads, nblock, GROUP), axis=2).transpose(1, 0, 2)
    lasts = cums[:, :, -1]
    block_decay = jnp.exp(lasts)
    total_decay = jnp.prod(block_decay, axis=0)
    tails = jnp.exp(lasts[:, :, None] - cums)
    head_ws = jnp.exp(cums)
    zero = jnp.zeros((heads, STATE, HEADDIM), jnp.float32)
    xw = (xs * tails.transpose(0, 2, 1)[..., None]).astype(jnp.bfloat16)
    summ = jnp.einsum("kqn,kqhp->khnp", bs, xw, preferred_element_type=jnp.float32)
    local_fwd = [zero]
    block = 0
    local_fwd.append(block_decay[block][:, None, None] * local_fwd[-1] + summ[block])
    incoming = carry_forward(total_decay, local_fwd[-1])
    running = jnp.ones((heads,), jnp.float32)
    block = 0
    incoming_state = [(local_fwd[block] + running[:, None, None] * incoming).astype(jnp.bfloat16)]
    gw = (gs * head_ws.transpose(0, 2, 1)[..., None]).astype(jnp.bfloat16)
    upd = jnp.einsum("kqn,kqhp->khnp", cs, gw, preferred_element_type=jnp.float32)
    local_bwd = [zero]
    local_bwd = local_bwd[::-1]
    before = upd[0] + block_decay[0][:, None, None] * local_bwd[0]
    leaving_state = carry_backward(total_decay, before)
    after = [None] * nblock
    running = jnp.ones((heads,), jnp.float32)
    block = 0
    after[block] = (local_bwd[block] + running[:, None, None] * leaving_state).astype(jnp.bfloat16)
    lower = jnp.arange(GROUP)[:, None] >= jnp.arange(GROUP)[None, :]
    block = 0
    cumk = cums[block]
    decay = jnp.where(
        lower[None], jnp.exp(jnp.minimum(cumk[:, :, None] - cumk[:, None, :], 0.0)), 0.0
    )
    mixed = jnp.einsum("qhp,shp->hqs", gs[block], xs[block], preferred_element_type=jnp.float32)
    first = (mixed * decay).astype(jnp.bfloat16)
    gram = jnp.dot(cs[block], bs[block].T, preferred_element_type=jnp.float32)
    third = (gram[None] * decay).astype(jnp.bfloat16)
    inter_c = jnp.einsum(
        "qhp,hnp->hqn", gs[block], incoming_state[block], preferred_element_type=jnp.float32
    )
    grad_c = jnp.einsum(
        "hqs,sn->qn", first, bs[block], preferred_element_type=jnp.float32
    ) + jnp.sum(head_ws[block][:, :, None] * inter_c, axis=0)
    inter_b = jnp.einsum(
        "qhp,hnp->hqn", xs[block], after[block], preferred_element_type=jnp.float32
    )
    grad_b = jnp.einsum(
        "hsq,sn->qn", first, cs[block], preferred_element_type=jnp.float32
    ) + jnp.sum(tails[block][:, :, None] * inter_b, axis=0)
    inter_x = jnp.einsum("qn,hnp->qhp", bs[block], after[block], preferred_element_type=jnp.float32)
    grad_x = (
        jnp.einsum("hsq,shp->qhp", third, gs[block], preferred_element_type=jnp.float32)
        + tails[block].T[:, :, None] * inter_x
    )
    pieces_x = grad_x.astype(jnp.bfloat16)
    grad_x_all = pieces_x.reshape(tokens, heads * HEADDIM)
    totals = lax.psum((grad_b, grad_c), "tp")
    rows = tokens // lax.axis_size("tp")
    offset = lax.axis_index("tp") * rows
    share_b = lax.dynamic_slice_in_dim(totals[0], offset, rows, 0)
    share_c = lax.dynamic_slice_in_dim(totals[1], offset, rows, 0)
    return (grad_x_all, share_b, share_c)


def solution(mesh):
    in_specs = (P("ctx", "tp"), P("tp", "ctx"), P("ctx", None), P("ctx", None), P("ctx", "tp"))
    out_specs = (P("ctx", "tp"), P(("ctx", "tp"), None), P(("ctx", "tp"), None))
    return jax.shard_map(shards, mesh=mesh, in_specs=in_specs, out_specs=out_specs, check_vma=False)
```

profile of v0, /device:TPU:1, one launch (start us, length us, event | category | flops | bytes accessed | tf_op | source)
XLA Modules:
  0.0 551.4 jit_solution(860969700310247095)
XLA Ops:
  8.9 1.1 copy.78
  10.3 1.8 fusion.15
  13.8 45.4 %all-gather = f32[64,10,1]{1,2,0:T(1,128)} all-gather(f32[1,10,1]{1,2,0:T(1,128)S(1)} %get-tuple-element.358), channel_id=2, replica_groups=mesh['ctx'=64,'tp'=8] {'ctx'}, dimensions={0}, use_global_device_ids=true | all-gather | bytes 2600 | tf_op jit(solution)/shard_map/all_gather | solution.py:13
  61.9 115.7 %all-gather.4.cloned.1.call-done = f32[64,10,128,64]{2,3,1,0:T(8,128)} async-done(((f32[1,10,128,64]{2,3,1,0:T(8,128)}), f32[64,10,128,64]{2,3,1,0:T(8,128)}) %all-gather.4.cloned.1.call-update) | async-done | bytes 20971536 | tf_op jit(solution)/shard_map/all_gather | solution.py:13
  177.7 135.1 %while.30 = (s32[]{:T(128)}, f32[10,128,64]{2,1,0:T(8,128)S(1)}, s32[]{:T(128)}, f32[64,10]{1,0:T(8,128)}, f32[64,10,128,64]{2,3,1,0:T(8,128)}, /*index=5*/s32[]{:T(128)}, s32[]{:T(128)}, s32[]{:T(128)}, s32[]{:T(128)}) while((s32[]{:T(128)}, f32[10,128,64]{2,1,0:T(8,128)S(1)}, s32[]{:T(128)}, f32[64,10]{1,0:T(8,128)}, ...), condition=%wide.region_3.4_spmd.clone, body=%wide.region_2.3_spmd.clone.sunk | while | flops 327688 | bytes 2294055 | solution.py:24
  200.8 1.0 constant_dynamic-slice_fusion.6
  236.6 1.1 constant_dynamic-slice_fusion.6
  245.1 1.0 constant_dynamic-slice_fusion.6
  255.7 1.0 constant_dynamic-slice_fusion.6
  266.2 1.0 constant_dynamic-slice_fusion.6
  268.3 1.0 constant_dynamic-slice_fusion.6
  272.6 1.0 constant_dynamic-slice_fusion.6
  283.1 1.0 constant_dynamic-slice_fusion.6
  287.3 1.0 constant_dynamic-slice_fusion.6
  289.5 1.0 constant_dynamic-slice_fusion.6
  297.9 1.0 constant_dynamic-slice_fusion.6
  300.1 1.0 constant_dynamic-slice_fusion.6
  304.3 1.0 constant_dynamic-slice_fusion.6
  310.7 1.0 constant_dynamic-slice_fusion.6
  314.1 24.8 %all-gather.6.cloned.1.call-done = f32[64,10,128,64]{2,3,1,0:T(8,128)} async-done(((f32[1,10,128,64]{2,3,1,0:T(8,128)}), f32[64,10,128,64]{2,3,1,0:T(8,128)}) %all-gather.6.cloned.1.call-update) | async-done | bytes 20971536 | tf_op jit(solution)/shard_map/all_gather | solution.py:13
  338.9 134.3 %while.31 = (s32[]{:T(128)}, f32[10,128,64]{2,1,0:T(8,128)S(1)}, s32[]{:T(128)}, f32[64,10]{1,0:T(8,128)}, f32[64,10,128,64]{2,3,1,0:T(8,128)}, /*index=5*/s32[]{:T(128)}, s32[]{:T(128)}) while((s32[]{:T(128)}, f32[10,128,64]{2,1,0:T(8,128)S(1)}, s32[]{:T(128)}, f32[64,10]{1,0:T(8,128)}, f32[64,10,128,64]{2,3,1,0:T(8,128)}, ...), condition=%wide.region_8.9_spmd.clone, body=%wide.region_7.8_spmd.clone.sunk | while | flops 327684 | bytes 2293993 | solution.py:24
  338.9 1.1 constant_dynamic-slice_fusion.7
  477.1 66.4 %all-reduce.3.cloned.1.call-done = (f32[256,128]{1,0:T(8,128)}, f32[256,128]{1,0:T(8,128)}) async-done(((f32[256,128]{1,0:T(8,128)}, f32[256,128]{1,0:T(8,128)}), (f32[256,128]{1,0:T(8,128)}, f32[256,128]{1,0:T(8,128)})) %all-reduce.3.cloned.1.call-update) | async-done | bytes 262160 | tf_op jit(solution)/shard_map/psum | solution.py:104
  543.6 1.3 constant_dynamic-slice_fusion.2
  (559 shorter events, 261.2 us)
Async XLA Ops:
  7.2 5.4 copy-start
  7.2 5.0 copy-start.3
  7.2 170.5 %all-gather.4.cloned.1.call-start = ((), (), s32[]{:S(2)}) async-start(), calls=%async_computation | async-start | bytes 21299200 | tf_op jit(solution)/shard_map/all_gather | solution.py:13
  10.1 49.9 %copy-start.1 = (bf16[256,128]{1,0:T(8,128)(2,1)S(1)}, bf16[256,128]{1,0:T(8,128)(2,1)}, u32[]{:S(2)}) copy-start(bf16[256,128]{1,0:T(8,128)(2,1)} %param.12) | copy-start | bytes 196612
  12.1 326.7 %all-gather.6.cloned.1.call-start = ((), (), s32[]{:S(2)}) async-start(), calls=%async_computation.1 | async-start | bytes 21299200 | tf_op jit(solution)/shard_map/all_gather | solution.py:13
  13.6 529.9 %all-reduce.3.cloned.1.call-start = ((), (), s32[]{:S(2)}) async-start(), calls=%async_computation.2 | async-start | bytes 524288 | tf_op jit(solution)/shard_map/psum | solution.py:104
  59.3 2.6 copy-start.6
  338.9 134.3 %copy-start.5 = (f32[10,256]{1,0:T(8,128)S(1)}, f32[10,256]{1,0:T(8,128)}, u32[]{:S(2)}) copy-start(f32[10,256]{1,0:T(8,128)} %get-tuple-element.354) | copy-start | bytes 30724
  338.9 134.7 %copy-start.2 = (f32[128,256]{0,1:T(8,128)S(1)}, f32[128,256]{0,1:T(8,128)}, u32[]{:S(2)}) copy-start(f32[128,256]{0,1:T(8,128)} %copy.89) | copy-start | bytes 393220
  338.9 136.5 %copy-start.4 = (f32[256,256]{1,0:T(8,128)S(1)}, f32[256,256]{1,0:T(8,128)}, u32[]{:S(2)}) copy-start(f32[256,256]{1,0:T(8,128)} %fusion.28) | copy-start | bytes 786436
  338.9 136.5 %copy-start.7 = (pred[256,256]{1,0:T(8,128)(4,1)S(1)}, pred[256,256]{1,0:T(8,128)(4,1)}, u32[]{:S(2)}) copy-start(pred[256,256]{1,0:T(8,128)(4,1)} %copy-done.6) | copy-start | bytes 196612
Sparse Core Ops, SparseCore 0:
  12.3 165.3 all-gather.3
  180.7 158.1 all-gather.5
  475.5 68.0 all-reduce.2
where the time goes:
time: 561 us; the launch traced here: 551 us
  local copies, waits for them, and re-layouts  252 us (45%)
  waiting for transfers between devices  207 us (37%)
  blocking collectives  45.4 us (8%)
  other arithmetic  20.1 us (4%)
  between operations  14 us (2%)
  matrix products  8.11 us (1%)
    dynamic_slice x256, local copies, waits for them, and re-layouts, step(): new = combine(before, jax.tree.map(lambda part: part[at], everything))  158 us
    all_gather x2, waiting for transfers between devices, carried_in(): everything = jax.tree.map(lambda part: lax.all_gather(part, axis), x)  141 us
    mul x128, local copies, waits for them, and re-layouts, link(): later[0][:, None, None] * earlier[1] + later[1]  88.3 us
    psum x1, waiting for transfers between devices, shards(): totals = lax.psum((grad_b, grad_c), 'tp')  66.4 us
    all_gather x1, blocking collectives, carried_in(): everything = jax.tree.map(lambda part: lax.all_gather(part, axis), x)  45.4 us
    select_n x128, other arithmetic, step(): return jax.tree.map(lambda a, b: jnp.where(reached, a, b), new, before)  18.5 us
  transfers between devices with their start and end apart: 3, of which 3 were waited for; matrix products, arithmetic and copies ran while one was open for 25% of the time, Pallas kernels for 0%

commit v1 on v0

v1 whole, which is shorter than its diff:
```python
import functools

import jax
import jax.numpy as jnp
from jax import lax
from jax.experimental import pallas as pl
from jax.experimental.pallas import tpu as pltpu
from jax.sharding import PartitionSpec as P

HEADDIM = 64
STATE = 128
GROUP = 256
HALVES = 2
FORWARD, BACKWARD = 0, 1
MESH = pl.DeviceIdType.MESH
F32, BF16 = jnp.float32, jnp.bfloat16
NT = (((1,), (1,)), ((), ()))


def grid_of(blocks):
    rows = 1
    while rows * rows < blocks:
        rows *= 2
    return blocks // rows, rows


def ring_offset(step, size):
    return size // 2 + ((step + 1) // 2) * (2 * (step % 2) - 1)


def kernel(
    ny, nz, nt,
    x_hbm, ld_hbm, b_hbm, c_hbm, g_hbm,
    gx_hbm, gb_out, gc_out,
    x_v, ld_v, b_v, c_v, g_v, xw_v, gw_v, tail_v, cols_v, row_v,
    own_dec, dec_z, dec_y, own_row, edge,
    states, rec_z, pre, total, rec_y, back, ret, hbf,
    acc_f, gx_acc, gx_bf, part, rec_t,
    load_sem, out_sem,
    dz_send, dz_recv, dy_send, dy_recv, z_send, z_recv, y_send, y_recv, r_send, r_recv, t_send, t_recv,
):
    heads = ld_v.shape[0]
    width = x_v.shape[1]
    pairs = width // 128
    piece = STATE // nz
    half = piece // HALVES
    rows = GROUP // nt
    me = lax.axis_index("ctx")
    me_t = lax.axis_index("tp")
    me_y, me_z = me // nz, lax.rem(me, nz)

    def at_z(z):
        return {"ctx": me_y * nz + z}

    def at_y(y):
        return {"ctx": y * nz + me_z}

    def at_t(t):
        return {"tp": t}

    loads = [
        pltpu.make_async_copy(src, dst, load_sem.at[i])
        for i, (src, dst) in enumerate(
            ((ld_hbm, ld_v), (b_hbm, b_v), (x_hbm, x_v), (c_hbm, c_v), (g_hbm, g_v))
        )
    ]
    for load in loads:
        load.start()

    barrier = pltpu.get_barrier_semaphore()

    def greet(to, size, mine):
        def body(i, carry):
            pl.semaphore_signal(
                barrier, inc=1, device_id=to(lax.rem(mine + 1 + i, size)), device_id_type=MESH
            )
            return carry

        lax.fori_loop(0, size - 1, body, 0)

    greet(at_z, nz, me_z)
    greet(at_y, ny, me_y)
    greet(at_t, nt, me_t)

    loads[0].wait()
    ld = ld_v[...]
    at_r = lax.broadcasted_iota(jnp.int32, (GROUP, GROUP), 0)
    at_c = lax.broadcasted_iota(jnp.int32, (GROUP, GROUP), 1)
    upper = (at_r <= at_c).astype(F32)
    lower = (at_r >= at_c).astype(F32)
    high = lax.Precision.HIGHEST
    row_v[...] = jnp.dot(ld, upper, precision=high, preferred_element_type=F32)
    cum_t = lax.dot_general(lower, ld, NT, precision=high, preferred_element_type=F32)
    lane = lax.broadcasted_iota(jnp.int32, (GROUP, 128), 1)
    left = lane < HEADDIM
    for h in range(heads):
        cols_v[h] = jnp.broadcast_to(cum_t[:, h : h + 1], (GROUP, 128))

    loads[1].wait()
    loads[2].wait()
    for p in range(pairs):
        at = slice(p * 128, p * 128 + 128)
        cum = jnp.where(left, cols_v[2 * p], cols_v[2 * p + 1])
        last = cum[GROUP - 1 : GROUP, :]
        tail = jnp.exp(last - cum)
        tail_v[:, at] = tail
        xw_v[:, at] = (x_v[:, at].astype(F32) * tail).astype(BF16)
        own_dec[:, at] = jnp.exp(last)
    bt = b_v[...].astype(F32).T.astype(BF16)
    states[FORWARD] = jnp.dot(bt, xw_v[...], preferred_element_type=F32)

    pl.semaphore_wait(barrier, nz + ny + nt - 3)

    def over(size, fn):
        def body(i, carry):
            fn(i)
            return carry

        lax.fori_loop(0, size, body, 0)

    def dec_z_copy(i):
        to = lax.rem(me_z + ring_offset(i, nz), nz)
        return pltpu.make_async_remote_copy(
            own_dec, dec_z.at[me_z], dz_send.at[to], dz_recv.at[me_z], at_z(to), MESH
        )

    def z_copy(way, part_at, i):
        to = lax.rem(me_z + ring_offset(i, nz), nz)
        chunk = way * HALVES + part_at
        return pltpu.make_async_remote_copy(
            states.at[way, pl.ds(pl.multiple_of(to * piece + part_at * half, half), half)],
            rec_z.at[way, part_at, me_z],
            z_send.at[chunk, to],
            z_recv.at[chunk, me_z],
            at_z(to),
            MESH,
        )

    def keep_own(way):
        for part_at in range(HALVES):
            rec_z[way, part_at, me_z] = states[
                way, pl.ds(pl.multiple_of(me_z * piece + part_at * half, half), half)
            ]

    over(nz - 1, lambda i: dec_z_copy(i).start())
    for part_at in range(HALVES):
        over(nz - 1, lambda i: z_copy(FORWARD, part_at, i).start())
    dec_z[me_z] = own_dec[...]
    keep_own(FORWARD)

    loads[3].wait()
    loads[4].wait()
    for p in range(pairs):
        at = slice(p * 128, p * 128 + 128)
        cum = jnp.where(left, cols_v[2 * p], cols_v[2 * p + 1])
        gw_v[:, at] = (g_v[:, at].astype(F32) * jnp.exp(cum)).astype(BF16)
    ct = c_v[...].astype(F32).T.astype(BF16)
    states[BACKWARD] = jnp.dot(ct, gw_v[...], preferred_element_type=F32)
    for part_at in range(HALVES):
        over(nz - 1, lambda i: z_copy(BACKWARD, part_at, i).start())
    keep_own(BACKWARD)

    gram_t = lax.dot_general(b_v[...], c_v[...], NT, preferred_element_type=F32)
    hb = GROUP // 2
    tri = (
        lax.broadcasted_iota(jnp.int32, (hb, hb), 0) <= lax.broadcasted_iota(jnp.int32, (hb, hb), 1)
    )
    lane_b = lax.broadcasted_iota(jnp.int32, (1, 128), 1)
    sides = ((lane_b < HEADDIM).astype(BF16), (lane_b >= HEADDIM).astype(BF16))
    tiles = ((0, 0), (0, 1), (1, 1))
    for p in range(pairs):
        at = slice(p * 128, p * 128 + 128)
        xp, gp = x_v[:, at], g_v[:, at]
        out = [jnp.zeros((hb, 128), F32) for _ in range(2)]
        for side in range(2):
            h = 2 * p + side
            gm = gp * sides[side]
            for ib, ub in tiles:
                mi, mu = slice(ib * hb, ib * hb + hb), slice(ub * hb, ub * hb + hb)
                mixed_t = lax.dot_general(xp[mi], gm[mu], NT, preferred_element_type=F32)
                decay_t = jnp.exp(jnp.minimum(row_v[h : h + 1, mu] - cols_v[h, mi, :], 0.0))
                if ib == ub:
                    decay_t = jnp.where(tri, decay_t, 0.0)
                first_t = mixed_t * decay_t
                if h == 0:
                    acc_f[mi, mu] = first_t
                else:
                    acc_f[mi, mu] += first_t
                third_t = (gram_t[mi, mu] * decay_t).astype(BF16)
                out[ib] = out[ib] + jnp.dot(third_t, gm[mu], preferred_element_type=F32)
        gx_acc[:hb, at] = out[0]
        gx_acc[hb:, at] = out[1]
    acc_f[hb:, :hb] = jnp.zeros((hb, hb), F32)
    first_t = acc_f[...]
    part[1] = jnp.dot(first_t.astype(BF16), c_v[...], preferred_element_type=F32)
    part[0] = jnp.dot(first_t.T.astype(BF16), b_v[...], preferred_element_type=F32)

    def wait_dec(i):
        src = lax.rem(me_z + ring_offset(i, nz), nz)
        pltpu.make_async_remote_copy(
            own_dec, dec_z.at[src], dz_send.at[src], dz_recv.at[src], at_z(src), MESH
        ).wait_recv()

    over(nz - 1, wait_dec)
    ahead = jnp.ones((1, width), F32)
    for z in range(nz):
        edge[FORWARD, z] = ahead
        ahead = ahead * dec_z[z]
    own_row[...] = ahead
    behind = jnp.ones((1, width), F32)
    for z in reversed(range(nz)):
        edge[BACKWARD, z] = behind
        behind = behind * dec_z[z]

    def dec_y_copy(i):
        to = lax.rem(me_y + ring_offset(i, ny), ny)
        return pltpu.make_async_remote_copy(
            own_row, dec_y.at[me_y], dy_send.at[to], dy_recv.at[me_y], at_y(to), MESH
        )

    over(ny - 1, lambda i: dec_y_copy(i).start())

    def y_copy(way, part_at, y):
        chunk = way * HALVES + part_at
        return pltpu.make_async_remote_copy(
            total.at[way, part_at],
            rec_y.at[way, part_at, me_y],
            y_send.at[chunk, y],
            y_recv.at[chunk, me_y],
            at_y(y),
            MESH,
        )

    def y_from(way, part_at, y):
        chunk = way * HALVES + part_at
        return pltpu.make_async_remote_copy(
            total.at[way, part_at],
            rec_y.at[way, part_at, y],
            y_send.at[chunk, y],
            y_recv.at[chunk, y],
            at_y(y),
            MESH,
        )

    def y_targets(way, fn):
        def body(y, carry):
            fn(y)
            return carry

        if way == FORWARD:
            lax.fori_loop(me_y + 1, ny, body, 0)
        else:
            lax.fori_loop(0, me_y, body, 0)

    def z_from(way, part_at, i):
        src = lax.rem(me_z + ring_offset(i, nz), nz)
        chunk = way * HALVES + part_at
        return pltpu.make_async_remote_copy(
            states.at[way, pl.ds(0, half)],
            rec_z.at[way, part_at, src],
            z_send.at[chunk, src],
            z_recv.at[chunk, src],
            at_z(src),
            MESH,
        )

    def scan_row(way, part_at):
        over(nz - 1, lambda i: z_from(way, part_at, i).wait_recv())
        state = jnp.zeros((half, width), F32)
        for z in range(nz) if way == FORWARD else reversed(range(nz)):
            pre[way, part_at, z] = state
            state = state * dec_z[z] + rec_z[way, part_at, z]
        total[way, part_at] = state
        y_targets(way, lambda y: y_copy(way, part_at, y).start())

    def ret_copy(way, part_at, i):
        to = lax.rem(me_z + ring_offset(i, nz), nz)
        chunk = way * HALVES + part_at
        return pltpu.make_async_remote_copy(
            back.at[way, part_at, to],
            ret.at[way, part_at, me_z],
            r_send.at[chunk, to],
            r_recv.at[chunk, me_z],
            at_z(to),
            MESH,
        )

    def ret_from(way, part_at, i):
        src = lax.rem(me_z + ring_offset(i, nz), nz)
        chunk = way * HALVES + part_at
        return pltpu.make_async_remote_copy(
            back.at[way, part_at, src],
            ret.at[way, part_at, src],
            r_send.at[chunk, src],
            r_recv.at[chunk, src],
            at_z(src),
            MESH,
        )

    def carry_row(way, part_at):
        def body(i, state):
            y = i if way == FORWARD else ny - 1 - i
            y_from(way, part_at, y).wait_recv()
            return state * dec_y[y] + rec_y[way, part_at, y]

        steps = me_y if way == FORWARD else ny - 1 - me_y
        state = lax.fori_loop(0, steps, body, jnp.zeros((half, width), F32))
        for z in range(nz):
            back[way, part_at, z] = pre[way, part_at, z] + edge[way, z] * state
        over(nz - 1, lambda i: ret_copy(way, part_at, i).start())
        ret[way, part_at, me_z] = back[way, part_at, me_z]

    scan_row(FORWARD, 0)
    scan_row(FORWARD, 1)

    def wait_dec_y(i):
        src = lax.rem(me_y + ring_offset(i, ny), ny)
        pltpu.make_async_remote_copy(
            own_row, dec_y.at[src], dy_send.at[src], dy_recv.at[src], at_y(src), MESH
        ).wait_recv()

    over(ny - 1, wait_dec_y)
    carry_row(FORWARD, 0)
    scan_row(BACKWARD, 0)
    carry_row(FORWARD, 1)
    scan_row(BACKWARD, 1)
    carry_row(BACKWARD, 0)
    carry_row(BACKWARD, 1)

    def collect(way):
        for part_at in range(HALVES):
            over(nz - 1, lambda i: ret_from(way, part_at, i).wait_recv())
        for z in range(nz):
            both = jnp.concatenate([ret[way, part_at, z] for part_at in range(HALVES)], axis=0)
            hbf[way, z * piece : z * piece + piece] = both.astype(BF16)

    def t_copy(way, i):
        to = lax.rem(me_t + 1 + i, nt)
        return pltpu.make_async_remote_copy(
            part.at[way, pl.ds(pl.multiple_of(to * rows, rows), rows)],
            rec_t.at[way, me_t],
            t_send.at[way, to],
            t_recv.at[way, me_t],
            at_t(to),
            MESH,
        )

    def t_from(way, i):
        src = lax.rem(me_t + 1 + i, nt)
        return pltpu.make_async_remote_copy(
            part.at[way, pl.ds(0, rows)],
            rec_t.at[way, src],
            t_send.at[way, src],
            t_recv.at[way, src],
            at_t(src),
            MESH,
        )

    def share(way):
        over(nt - 1, lambda i: t_copy(way, i).start())
        rec_t[way, me_t] = part[way, pl.ds(pl.multiple_of(me_t * rows, rows), rows)]

    collect(FORWARD)
    part[0] += lax.dot_general(gw_v[...], hbf[FORWARD], NT, preferred_element_type=F32)
    share(0)
    collect(BACKWARD)
    part[1] += lax.dot_general(xw_v[...], hbf[BACKWARD], NT, preferred_element_type=F32)
    share(1)
    inter = jnp.dot(b_v[...], hbf[BACKWARD], preferred_element_type=F32)
    gx_bf[...] = (gx_acc[...] + tail_v[...] * inter).astype(BF16)
    store = pltpu.make_async_copy(gx_bf, gx_hbm, out_sem)
    store.start()

    for way, out in ((0, gc_out), (1, gb_out)):
        over(nt - 1, lambda i: t_from(way, i).wait_recv())
        out[...] = jnp.sum(rec_t[way], axis=0)

    over(nz - 1, lambda i: dec_z_copy(i).wait_send())
    over(ny - 1, lambda i: dec_y_copy(i).wait_send())
    for way in (FORWARD, BACKWARD):
        for part_at in range(HALVES):
            over(nz - 1, lambda i: z_copy(way, part_at, i).wait_send())
            y_targets(way, lambda y: y_copy(way, part_at, y).wait_send())
            over(nz - 1, lambda i: ret_copy(way, part_at, i).wait_send())
    for way in range(2):
        over(nt - 1, lambda i: t_copy(way, i).wait_send())
    store.wait()


def shards(x_heads, log_decay, b_proj, c_proj, grad_out):
    blocks, nt = lax.axis_size("ctx"), lax.axis_size("tp")
    ny, nz = grid_of(blocks)
    heads = log_decay.shape[0]
    width = heads * HEADDIM
    piece = STATE // nz
    half = piece // HALVES
    rows = GROUP // nt
    chunks = 2 * HALVES
    anywhere = pl.BlockSpec(memory_space=pl.ANY)
    in_vmem = pl.BlockSpec(memory_space=pltpu.VMEM)
    dma = pltpu.SemaphoreType.DMA
    vmem = pltpu.VMEM
    grad_x, grad_b, grad_c = pl.pallas_call(
        functools.partial(kernel, ny, nz, nt),
        out_shape=(
            jax.ShapeDtypeStruct((GROUP, width), BF16),
            jax.ShapeDtypeStruct((rows, STATE), F32),
            jax.ShapeDtypeStruct((rows, STATE), F32),
        ),
        in_specs=[anywhere] * 5,
        out_specs=(anywhere, in_vmem, in_vmem),
        scratch_shapes=[
            vmem((GROUP, width), BF16),
            vmem((heads, GROUP), F32),
            vmem((GROUP, STATE), BF16),
            vmem((GROUP, STATE), BF16),
            vmem((GROUP, width), BF16),
            vmem((GROUP, width), BF16),
            vmem((GROUP, width), BF16),
            vmem((GROUP, width), F32),
            vmem((heads, GROUP, 128), F32),
            vmem((heads, GROUP), F32),
            vmem((1, width), F32),
            vmem((nz, 1, width), F32),
            vmem((ny, 1, width), F32),
            vmem((1, width), F32),
            vmem((2, nz, 1, width), F32),
            vmem((2, STATE, width), F32),
            vmem((2, HALVES, nz, half, width), F32),
            vmem((2, HALVES, nz, half, width), F32),
            vmem((2, HALVES, half, width), F32),
            vmem((2, HALVES, ny, half, width), F32),
            vmem((2, HALVES, nz, half, width), F32),
            vmem((2, HALVES, nz, half, width), F32),
            vmem((2, STATE, width), BF16),
            vmem((GROUP, GROUP), F32),
            vmem((GROUP, width), F32),
            vmem((GROUP, width), BF16),
            vmem((2, GROUP, STATE), F32),
            vmem((2, nt, rows, STATE), F32),
            dma((5,)),
            dma,
            dma((nz,)),
            dma((nz,)),
            dma((ny,)),
            dma((ny,)),
            dma((chunks, nz)),
            dma((chunks, nz)),
            dma((chunks, ny)),
            dma((chunks, ny)),
            dma((chunks, nz)),
            dma((chunks, nz)),
            dma((2, nt)),
            dma((2, nt)),
        ],
        compiler_params=pltpu.CompilerParams(
            collective_id=0, has_side_effects=True, vmem_limit_bytes=48 * 1024 * 1024
        ),
        name="mixer_backward",
    )(x_heads, log_decay, b_proj, c_proj, grad_out)
    return grad_x, grad_b, grad_c


def solution(mesh):
    in_specs = (P("ctx", "tp"), P("tp", "ctx"), P("ctx", None), P("ctx", None), P("ctx", "tp"))
    out_specs = (P("ctx", "tp"), P(("ctx", "tp"), None), P(("ctx", "tp"), None))
    return jax.shard_map(shards, mesh=mesh, in_specs=in_specs, out_specs=out_specs, check_vma=False)
```

time: 561 us -> 62.8 us (0.11); the launches traced: 551 us -> 62.5 us
  local copies, waits for them, and re-layouts: 252 us -> 6.27 us
  waiting for transfers between devices: 207 us -> 0 us
  Pallas kernels: 0 us -> 55.6 us
  blocking collectives: 45.4 us -> 0 us
  other arithmetic: 20.1 us -> 0 us
  between operations: 14 us -> 0.65 us
  matrix products: 8.11 us -> 0 us
    dynamic_slice x257 -> x0, local copies, waits for them, and re-layouts: 160 us -> none  [the longest x256 158 us: step(): new = combine(before, jax.tree.map(lambda part: part[at], everything))]
    all_gather x2 -> x0, waiting for transfers between devices: 141 us -> none  [carried_in(): everything = jax.tree.map(lambda part: lax.all_gather(part, axis), x)]
    mul x130 -> x0, local copies, waits for them, and re-layouts: 88.4 us -> none  [the longest x128 88.3 us: link(): later[0][:, None, None] * earlier[1] + later[1]]
    psum x1 -> x0, waiting for transfers between devices: 66.4 us -> none  [shards(): totals = lax.psum((grad_b, grad_c), 'tp')]
    pallas_call x0 -> x1, Pallas kernels: none -> 55.6 us  [shards(): pl.pallas_call(functools.partial(kernel, ny, nz, nt), out_shape=(jax.Shap...]
    all_gather x1 -> x0, blocking collectives: 45.4 us -> none  [carried_in(): everything = jax.tree.map(lambda part: lax.all_gather(part, axis), x)]
    select_n x128 -> x0, other arithmetic: 18.5 us -> none  [step(): return jax.tree.map(lambda a, b: jnp.where(reached, a, b), new, before)]
    dot_general x10 -> x0, matrix products: 8.11 us -> none  [the longest x1 1.81 us: shards(): jnp.einsum('kqn,kqhp->khnp', cs, gw, preferred_element_type=jnp.float32)]
  transfers between devices with their start and end apart: 3 -> 0, of which waited for: 3 -> 0; matrix products, arithmetic and copies ran while one was open for 25% -> 0% of each run, Pallas kernels for 0% -> 0%
where the time goes in v1:
time: 62.8 us; the launch traced here: 62.5 us
  Pallas kernels  55.6 us (89%)
  local copies, waits for them, and re-layouts  6.27 us (10%)
  between operations  0.65 us (1%)
    pallas_call x1, Pallas kernels, shards(): pl.pallas_call(functools.partial(kernel, ny, nz, nt), out_shape=(jax.Shap...  55.6 us
    unnamed x13, local copies, waits for them, and re-layouts  6.27 us

profile of v1, /device:TPU:1, one launch (start us, length us, event | category | flops | bytes accessed | tf_op | source)
XLA Modules:
  0.0 62.5 jit_solution(17828707656772806613)
XLA Ops:
  0.6 0.0 copy-start
  0.6 1.0 %copy-done = bf16[256,640]{1,0:T(8,128)(2,1)S(1)} copy-done((bf16[256,640]{1,0:T(8,128)(2,1)S(1)}, bf16[256,640]{1,0:T(8,128)(2,1)}, u32[]{:S(2)}) %copy-start) | copy-done | bytes 327704
  1.6 0.0 copy-start.1
  1.6 1.0 %copy-done.1 = bf16[256,640]{1,0:T(8,128)(2,1)S(1)} copy-done((bf16[256,640]{1,0:T(8,128)(2,1)S(1)}, bf16[256,640]{1,0:T(8,128)(2,1)}, u32[]{:S(2)}) %copy-start.1) | copy-done | bytes 327704
  2.6 0.0 copy-start.2
  2.6 0.8 %copy-done.2 = bf16[256,128]{1,0:T(8,128)(2,1)S(1)} copy-done((bf16[256,128]{1,0:T(8,128)(2,1)S(1)}, bf16[256,128]{1,0:T(8,128)(2,1)}, u32[]{:S(2)}) %copy-start.2) | copy-done | bytes 65560
  3.4 0.0 copy-start.3
  3.4 0.8 %copy-done.3 = bf16[256,128]{1,0:T(8,128)(2,1)S(1)} copy-done((bf16[256,128]{1,0:T(8,128)(2,1)S(1)}, bf16[256,128]{1,0:T(8,128)(2,1)}, u32[]{:S(2)}) %copy-start.3) | copy-done | bytes 65560
  4.3 0.0 copy-start.4
  4.3 0.7 %copy-done.4 = f32[10,256]{1,0:T(8,128)S(1)} copy-done((f32[10,256]{1,0:T(8,128)S(1)}, f32[10,256]{1,0:T(8,128)}, u32[]{:S(2)}) %copy-start.4) | copy-done | bytes 10264
  5.0 55.6 %mixer_backward.1 = (bf16[256,640]{1,0:T(8,128)(2,1)S(1)}, f32[32,128]{1,0:T(8,128)S(1)}, f32[32,128]{1,0:T(8,128)S(1)}) custom-call(bf16[256,640]{1,0:T(8,128)(2,1)S(1)} %copy-done, f32[10,256]{1,0:T(8,128)S(1)} %copy-done.4, bf16[256,128]{1,0:T(8,128)(2,1)S(1)} %copy-done.2, bf16[256,128]{1,0:T(8,128)(2,1)S(1)} %copy-done.3, bf16[256,640]{1,0:T(8,128)(2,1)S(1)} %copy-done.1), custom_call_target="tpu_custom_call" | custom-call | tf_op jit(solution)/shard_map/mixer_backward/pallas_call | solution.py:403
  60.6 0.7 %copy.11 = bf16[256,640]{1,0:T(8,128)(2,1)} copy(bf16[256,640]{1,0:T(8,128)(2,1)S(1)} %get-tuple-element.6) | data formatting | bytes 655360
  61.3 0.6 copy.12
  61.9 0.6 copy.13
Async XLA Ops:
  0.6 1.0 %copy-start = (bf16[256,640]{1,0:T(8,128)(2,1)S(1)}, bf16[256,640]{1,0:T(8,128)(2,1)}, u32[]{:S(2)}) copy-start(bf16[256,640]{1,0:T(8,128)(2,1)} %x_hbm.1) | copy-start | bytes 983044
  1.6 1.0 %copy-start.1 = (bf16[256,640]{1,0:T(8,128)(2,1)S(1)}, bf16[256,640]{1,0:T(8,128)(2,1)}, u32[]{:S(2)}) copy-start(bf16[256,640]{1,0:T(8,128)(2,1)} %g_hbm.1) | copy-start | bytes 983044
  2.6 0.8 %copy-start.2 = (bf16[256,128]{1,0:T(8,128)(2,1)S(1)}, bf16[256,128]{1,0:T(8,128)(2,1)}, u32[]{:S(2)}) copy-start(bf16[256,128]{1,0:T(8,128)(2,1)} %b_hbm.1) | copy-start | bytes 196612
  3.4 0.8 %copy-start.3 = (bf16[256,128]{1,0:T(8,128)(2,1)S(1)}, bf16[256,128]{1,0:T(8,128)(2,1)}, u32[]{:S(2)}) copy-start(bf16[256,128]{1,0:T(8,128)(2,1)} %c_hbm.1) | copy-start | bytes 196612
  4.3 0.7 %copy-start.4 = (f32[10,256]{1,0:T(8,128)S(1)}, f32[10,256]{1,0:T(8,128)}, u32[]{:S(2)}) copy-start(f32[10,256]{1,0:T(8,128)} %ld_hbm.1) | copy-start | bytes 30724

commit v2 on v1

v2 whole, which is shorter than its diff:
```python
import functools

import jax
import jax.numpy as jnp
from jax import lax
from jax.experimental import pallas as pl
from jax.experimental.pallas import tpu as pltpu
from jax.sharding import PartitionSpec as P

HEADDIM = 64
STATE = 128
GROUP = 256
HALVES = 2
FORWARD, BACKWARD = 0, 1
MESH = pl.DeviceIdType.MESH
F32, BF16 = jnp.float32, jnp.bfloat16
NT = (((1,), (1,)), ((), ()))


def grid_of(blocks):
    rows = 1
    while rows * rows < blocks:
        rows *= 2
    return blocks // rows, rows


def ring_offsets(size):
    return [size // 2 + ((i + 1) // 2) * (2 * (i % 2) - 1) for i in range(size - 1)]


def wait_bytes(ref, sem):
    pltpu.make_async_copy(ref, ref, sem).wait()


def kernel(
    ny, nz, nt,
    x_hbm, ld_hbm, b_hbm, c_hbm, g_hbm,
    gx_out, gb_out, gc_out,
    x_v, ld_v, b_v, c_v, g_v, xw_v, gw_v, tail_v, cols_v, row_v,
    own_dec, dec_z, dec_y, own_row, edge,
    states, rec_z, pre, total, rec_y, back, ret, hbf,
    acc_f, gx_acc, part, rec_t,
    load_sem,
    dz_send, dz_recv, dy_send, dy_recv, z_send, z_recv, y_send, y_recv, r_send, r_recv, t_send, t_recv,
):
    heads = ld_v.shape[0]
    width = x_v.shape[1]
    pairs = width // 128
    piece = STATE // nz
    half = piece // HALVES
    rows = GROUP // nt
    me = lax.axis_index("ctx")
    me_t = lax.axis_index("tp")
    me_y, me_z = me // nz, lax.rem(me, nz)

    def at_z(z):
        return {"ctx": me_y * nz + z}

    def at_y(y):
        return {"ctx": y * nz + me_z}

    def at_t(t):
        return {"tp": t}

    loads = [
        pltpu.make_async_copy(src, dst, load_sem.at[i])
        for i, (src, dst) in enumerate(
            ((ld_hbm, ld_v), (b_hbm, b_v), (x_hbm, x_v), (c_hbm, c_v), (g_hbm, g_v))
        )
    ]
    for load in loads:
        load.start()

    barrier = pltpu.get_barrier_semaphore()

    z_to = [lax.rem(me_z + off, nz) for off in ring_offsets(nz)]
    z_up = [k + jnp.where(me_z <= k, 1, 0) for k in range(nz - 1)]
    y_to = [lax.rem(me_y + off, ny) for off in ring_offsets(ny)]
    t_to = [lax.rem(me_t + off, nt) for off in range(1, nt)]
    for to, peers in ((at_z, z_to), (at_y, y_to), (at_t, t_to)):
        for peer in peers:
            pl.semaphore_signal(barrier, inc=1, device_id=to(peer), device_id_type=MESH)

    loads[0].wait()
    ld = ld_v[...]
    at_r = lax.broadcasted_iota(jnp.int32, (GROUP, GROUP), 0)
    at_c = lax.broadcasted_iota(jnp.int32, (GROUP, GROUP), 1)
    lower = (at_r >= at_c).astype(F32)
    high = lax.Precision.HIGHEST
    cum_t = lax.dot_general(lower, ld, NT, precision=high, preferred_element_type=F32)
    lane = lax.broadcasted_iota(jnp.int32, (GROUP, 128), 1)
    left = lane < HEADDIM
    for h in range(heads):
        cols_v[h] = jnp.broadcast_to(cum_t[:, h : h + 1], (GROUP, 128))

    loads[1].wait()
    loads[2].wait()
    for p in range(pairs):
        at = slice(p * 128, p * 128 + 128)
        cum = jnp.where(left, cols_v[2 * p], cols_v[2 * p + 1])
        last = cum[GROUP - 1 : GROUP, :]
        tail = jnp.exp(last - cum)
        tail_v[:, at] = tail
        xw_v[:, at] = (x_v[:, at].astype(F32) * tail).astype(BF16)
        own_dec[:, at] = jnp.exp(last)
    bt = b_v[...].astype(F32).T.astype(BF16)
    states[FORWARD] = jnp.dot(bt, xw_v[...], preferred_element_type=F32)

    pl.semaphore_wait(barrier, nz + ny + nt - 3)

    def remote(src, dst, send, recv, to):
        return pltpu.make_async_remote_copy(src, dst, send, recv, to, MESH)

    for to in z_to:
        remote(own_dec, dec_z.at[me_z], dz_send, dz_recv, at_z(to)).start()

    def send_pieces(way):
        for part_at in range(HALVES):
            chunk = way * HALVES + part_at
            for to in z_to:
                remote(
                    states.at[way, pl.ds(pl.multiple_of(to * piece + part_at * half, half), half)],
                    rec_z.at[way, part_at, me_z],
                    z_send.at[chunk],
                    z_recv.at[chunk],
                    at_z(to),
                ).start()
        for part_at in range(HALVES):
            rec_z[way, part_at, me_z] = states[
                way, pl.ds(pl.multiple_of(me_z * piece + part_at * half, half), half)
            ]

    send_pieces(FORWARD)
    dec_z[me_z] = own_dec[...]

    loads[3].wait()
    loads[4].wait()
    for p in range(pairs):
        at = slice(p * 128, p * 128 + 128)
        cum = jnp.where(left, cols_v[2 * p], cols_v[2 * p + 1])
        gw_v[:, at] = (g_v[:, at].astype(F32) * jnp.exp(cum)).astype(BF16)
    ct = c_v[...].astype(F32).T.astype(BF16)
    states[BACKWARD] = jnp.dot(ct, gw_v[...], preferred_element_type=F32)
    send_pieces(BACKWARD)

    others_z, others_y, others_t = pl.ds(0, nz - 1), pl.ds(0, ny - 1), pl.ds(0, nt - 1)
    wait_bytes(dec_z.at[others_z], dz_recv)
    ahead = jnp.ones((1, width), F32)
    for z in range(nz):
        edge[FORWARD, z] = ahead
        ahead = ahead * dec_z[z]
    own_row[...] = ahead
    behind = jnp.ones((1, width), F32)
    for z in reversed(range(nz)):
        edge[BACKWARD, z] = behind
        behind = behind * dec_z[z]
    for to in y_to:
        remote(own_row, dec_y.at[me_y], dy_send, dy_recv, at_y(to)).start()

    upper = (at_r <= at_c).astype(F32)
    row_v[...] = jnp.dot(ld, upper, precision=high, preferred_element_type=F32)
    gram_t = lax.dot_general(b_v[...], c_v[...], NT, preferred_element_type=F32)
    hb = GROUP // 2
    tri = (
        lax.broadcasted_iota(jnp.int32, (hb, hb), 0) <= lax.broadcasted_iota(jnp.int32, (hb, hb), 1)
    )
    lane_b = lax.broadcasted_iota(jnp.int32, (1, 128), 1)
    sides = ((lane_b < HEADDIM).astype(BF16), (lane_b >= HEADDIM).astype(BF16))
    tiles = ((0, 0), (0, 1), (1, 1))
    for p in range(pairs):
        at = slice(p * 128, p * 128 + 128)
        xp, gp = x_v[:, at], g_v[:, at]
        out = [jnp.zeros((hb, 128), F32) for _ in range(2)]
        for side in range(2):
            h = 2 * p + side
            gm = gp * sides[side]
            for ib, ub in tiles:
                mi, mu = slice(ib * hb, ib * hb + hb), slice(ub * hb, ub * hb + hb)
                mixed_t = lax.dot_general(xp[mi], gm[mu], NT, preferred_element_type=F32)
                decay_t = jnp.exp(jnp.minimum(row_v[h : h + 1, mu] - cols_v[h, mi, :], 0.0))
                if ib == ub:
                    decay_t = jnp.where(tri, decay_t, 0.0)
                first_t = mixed_t * decay_t
                if h == 0:
                    acc_f[mi, mu] = first_t
                else:
                    acc_f[mi, mu] += first_t
                third_t = (gram_t[mi, mu] * decay_t).astype(BF16)
                out[ib] = out[ib] + jnp.dot(third_t, gm[mu], preferred_element_type=F32)
        gx_acc[:hb, at] = out[0]
        gx_acc[hb:, at] = out[1]
    acc_f[hb:, :hb] = jnp.zeros((hb, hb), F32)
    first_t = acc_f[...]
    part[1] = jnp.dot(first_t.astype(BF16), c_v[...], preferred_element_type=F32)
    part[0] = jnp.dot(first_t.T.astype(BF16), b_v[...], preferred_element_type=F32)

    def y_copy(way, part_at, y):
        chunk = way * HALVES + part_at
        return remote(
            total.at[way, part_at],
            rec_y.at[way, part_at, me_y],
            y_send.at[chunk, y],
            y_recv.at[chunk, me_y],
            at_y(y),
        )

    def y_from(way, part_at, y):
        chunk = way * HALVES + part_at
        return remote(
            total.at[way, part_at],
            rec_y.at[way, part_at, y],
            y_send.at[chunk, y],
            y_recv.at[chunk, y],
            at_y(y),
        )

    def y_targets(way, fn):
        def body(y, carry):
            fn(y)
            return carry

        if way == FORWARD:
            lax.fori_loop(me_y + 1, ny, body, 0)
        else:
            lax.fori_loop(0, me_y, body, 0)

    def scan_row(way, part_at):
        wait_bytes(rec_z.at[way, part_at, others_z], z_recv.at[way * HALVES + part_at])
        state = jnp.zeros((half, width), F32)
        for z in range(nz) if way == FORWARD else reversed(range(nz)):
            pre[way, part_at, z] = state
            state = state * dec_z[z] + rec_z[way, part_at, z]
        total[way, part_at] = state
        y_targets(way, lambda y: y_copy(way, part_at, y).start())

    def carry_row(way, part_at):
        def body(i, state):
            y = i if way == FORWARD else ny - 1 - i
            y_from(way, part_at, y).wait_recv()
            return state * dec_y[y] + rec_y[way, part_at, y]

        steps = me_y if way == FORWARD else ny - 1 - me_y
        state = lax.fori_loop(0, steps, body, jnp.zeros((half, width), F32))
        for z in range(nz):
            back[way, part_at, z] = pre[way, part_at, z] + edge[way, z] * state
        ret[way, part_at, me_z] = back[way, part_at, me_z]

    def give_back(way, part_at, targets):
        chunk = way * HALVES + part_at
        for to in targets:
            remote(
                back.at[way, part_at, to],
                ret.at[way, part_at, me_z],
                r_send.at[chunk],
                r_recv.at[chunk],
                at_z(to),
            ).start()

    cut = (nz - 1) // 2
    early, late = z_up[:cut], z_up[cut:]
    scan_row(FORWARD, 0)
    scan_row(FORWARD, 1)
    wait_bytes(dec_y.at[others_y], dy_recv)
    carry_row(FORWARD, 0)
    give_back(FORWARD, 0, early)
    scan_row(BACKWARD, 0)
    carry_row(FORWARD, 1)
    give_back(FORWARD, 1, early)
    give_back(FORWARD, 0, late)
    scan_row(BACKWARD, 1)
    carry_row(BACKWARD, 0)
    give_back(BACKWARD, 0, early)
    give_back(FORWARD, 1, late)
    carry_row(BACKWARD, 1)
    give_back(BACKWARD, 1, early)
    give_back(BACKWARD, 0, late)
    give_back(BACKWARD, 1, late)

    def collect(way):
        for part_at in range(HALVES):
            wait_bytes(ret.at[way, part_at, others_z], r_recv.at[way * HALVES + part_at])
        for z in range(nz):
            both = jnp.concatenate([ret[way, part_at, z] for part_at in range(HALVES)], axis=0)
            hbf[way, z * piece : z * piece + piece] = both.astype(BF16)

    def share(way):
        for to in t_to:
            remote(
                part.at[way, pl.ds(pl.multiple_of(to * rows, rows), rows)],
                rec_t.at[way, me_t],
                t_send.at[way],
                t_recv.at[way],
                at_t(to),
            ).start()
        rec_t[way, me_t] = part[way, pl.ds(pl.multiple_of(me_t * rows, rows), rows)]

    collect(FORWARD)
    part[0] += lax.dot_general(gw_v[...], hbf[FORWARD], NT, preferred_element_type=F32)
    share(0)
    collect(BACKWARD)
    part[1] += lax.dot_general(xw_v[...], hbf[BACKWARD], NT, preferred_element_type=F32)
    share(1)
    inter = jnp.dot(b_v[...], hbf[BACKWARD], preferred_element_type=F32)
    gx_out[...] = (gx_acc[...] + tail_v[...] * inter).astype(BF16)

    wait_bytes(dec_z.at[others_z], dz_send)
    wait_bytes(dec_y.at[others_y], dy_send)
    for way in (FORWARD, BACKWARD):
        for part_at in range(HALVES):
            chunk = way * HALVES + part_at
            wait_bytes(rec_z.at[way, part_at, others_z], z_send.at[chunk])
            wait_bytes(ret.at[way, part_at, others_z], r_send.at[chunk])
            y_targets(way, lambda y: y_copy(way, part_at, y).wait_send())
    for way, out in ((0, gc_out), (1, gb_out)):
        wait_bytes(rec_t.at[way, others_t], t_recv.at[way])
        out[...] = jnp.sum(rec_t[way], axis=0)
        wait_bytes(rec_t.at[way, others_t], t_send.at[way])


def write_kernel(gx, gb, gc, gx_hbm, gb_hbm, gc_hbm, sem):
    copies = [
        pltpu.make_async_copy(src, dst, sem.at[i])
        for i, (src, dst) in enumerate(((gx, gx_hbm), (gb, gb_hbm), (gc, gc_hbm)))
    ]
    for copy in copies:
        copy.start()
    for copy in copies:
        copy.wait()


def shards(x_heads, log_decay, b_proj, c_proj, grad_out):
    blocks, nt = lax.axis_size("ctx"), lax.axis_size("tp")
    ny, nz = grid_of(blocks)
    heads = log_decay.shape[0]
    width = heads * HEADDIM
    piece = STATE // nz
    half = piece // HALVES
    rows = GROUP // nt
    chunks = 2 * HALVES
    in_hbm = pl.BlockSpec(memory_space=pltpu.HBM)
    in_vmem = pl.BlockSpec(memory_space=pltpu.VMEM)
    dma = pltpu.SemaphoreType.DMA
    vmem = pltpu.VMEM
    inputs = (x_heads, log_decay, b_proj, c_proj, grad_out)
    inputs = [pltpu.with_memory_space_constraint(a, pltpu.HBM) for a in inputs]
    out_shape = (
        jax.ShapeDtypeStruct((GROUP, width), BF16),
        jax.ShapeDtypeStruct((rows, STATE), F32),
        jax.ShapeDtypeStruct((rows, STATE), F32),
    )
    results = pl.pallas_call(
        functools.partial(kernel, ny, nz, nt),
        out_shape=out_shape,
        in_specs=[in_hbm] * 5,
        out_specs=[in_vmem] * 3,
        scratch_shapes=[
            vmem((GROUP, width), BF16),
            vmem((heads, GROUP), F32),
            vmem((GROUP, STATE), BF16),
            vmem((GROUP, STATE), BF16),
            vmem((GROUP, width), BF16),
            vmem((GROUP, width), BF16),
            vmem((GROUP, width), BF16),
            vmem((GROUP, width), F32),
            vmem((heads, GROUP, 128), F32),
            vmem((heads, GROUP), F32),
            vmem((1, width), F32),
            vmem((nz, 1, width), F32),
            vmem((ny, 1, width), F32),
            vmem((1, width), F32),
            vmem((2, nz, 1, width), F32),
            vmem((2, STATE, width), F32),
            vmem((2, HALVES, nz, half, width), F32),
            vmem((2, HALVES, nz, half, width), F32),
            vmem((2, HALVES, half, width), F32),
            vmem((2, HALVES, ny, half, width), F32),
            vmem((2, HALVES, nz, half, width), F32),
            vmem((2, HALVES, nz, half, width), F32),
            vmem((2, STATE, width), BF16),
            vmem((GROUP, GROUP), F32),
            vmem((GROUP, width), F32),
            vmem((2, GROUP, STATE), F32),
            vmem((2, nt, rows, STATE), F32),
            dma((5,)),
            dma,
            dma,
            dma,
            dma,
            dma((chunks,)),
            dma((chunks,)),
            dma((chunks, ny)),
            dma((chunks, ny)),
            dma((chunks,)),
            dma((chunks,)),
            dma((2,)),
            dma((2,)),
        ],
        compiler_params=pltpu.CompilerParams(
            collective_id=0, has_side_effects=True, vmem_limit_bytes=48 * 1024 * 1024
        ),
        name="mixer_backward",
    )(*inputs)
    return pl.pallas_call(
        write_kernel,
        out_shape=out_shape,
        in_specs=[pl.BlockSpec(memory_space=pl.ANY)] * 3,
        out_specs=[in_hbm] * 3,
        scratch_shapes=[dma((3,))],
        compiler_params=pltpu.CompilerParams(vmem_limit_bytes=1024 * 1024),
        name="write_out",
    )(*results)


def solution(mesh):
    in_specs = (P("ctx", "tp"), P("tp", "ctx"), P("ctx", None), P("ctx", None), P("ctx", "tp"))
    out_specs = (P("ctx", "tp"), P(("ctx", "tp"), None), P(("ctx", "tp"), None))
    return jax.shard_map(shards, mesh=mesh, in_specs=in_specs, out_specs=out_specs, check_vma=False)
```

time: 62.8 us -> 52.9 us (0.84)
  local copies, waits for them, and re-layouts: 6.27 us -> 0 us
  Pallas kernels: 55.6 us -> 52.1 us
    unnamed x13 -> x0, local copies, waits for them, and re-layouts: 6.27 us -> none
    pallas_call x1 -> x2, Pallas kernels: 55.6 us -> 52.1 us  [the longest x1 51.3 us: shards(): pl.pallas_call(functools.partial(kernel, ny, nz, nt), out_shape=out_shape...]
where the time goes in v2:
time: 52.9 us; the launch traced here: 52.7 us
  Pallas kernels  52.1 us (98%)
  between operations  0.64 us (1%)
    pallas_call x1, Pallas kernels, shards(): pl.pallas_call(functools.partial(kernel, ny, nz, nt), out_shape=out_shape...  51.3 us

profile of v2, /device:TPU:1, one launch (start us, length us, event | category | flops | bytes accessed | tf_op | source)
XLA Modules:
  0.0 52.7 jit_solution(7705235548045116818)
XLA Ops:
  0.6 51.3 %mixer_backward.1 = (bf16[256,640]{1,0:T(8,128)(2,1)S(1)}, f32[32,128]{1,0:T(8,128)S(1)}, f32[32,128]{1,0:T(8,128)S(1)}) custom-call(bf16[256,640]{1,0:T(8,128)(2,1)} %x_hbm.1, f32[10,256]{1,0:T(8,128)} %ld_hbm.1, bf16[256,128]{1,0:T(8,128)(2,1)} %b_hbm.1, bf16[256,128]{1,0:T(8,128)(2,1)} %c_hbm.1, bf16[256,640]{1,0:T(8,128)(2,1)} %g_hbm.1), custom_call_target="tpu_custom_call" | custom-call | tf_op jit(solution)/shard_map/mixer_backward/pallas_call | solution.py:351
  52.0 0.8 %write_out.1 = (bf16[256,640]{1,0:T(8,128)(2,1)}, f32[32,128]{1,0:T(8,128)}, f32[32,128]{1,0:T(8,128)}) custom-call(bf16[256,640]{1,0:T(8,128)(2,1)S(1)} %get-tuple-element.6.gx, f32[32,128]{1,0:T(8,128)S(1)} %get-tuple-element.7.gb, f32[32,128]{1,0:T(8,128)S(1)} %get-tuple-element.8.gc), custom_call_target="tpu_custom_call" | custom-call | tf_op jit(solution)/shard_map/write_out/pallas_call | solution.py:403

commit v3 on v2

--- a/solution.py
+++ b/solution.py
@@ -76,7 +76,7 @@
     z_to = [lax.rem(me_z + off, nz) for off in ring_offsets(nz)]
     z_up = [k + jnp.where(me_z <= k, 1, 0) for k in range(nz - 1)]
     y_to = [lax.rem(me_y + off, ny) for off in ring_offsets(ny)]
-    t_to = [lax.rem(me_t + off, nt) for off in range(1, nt)]
+    t_to = [lax.rem(me_t + off, nt) for off in ring_offsets(nt)]
     for to, peers in ((at_z, z_to), (at_y, y_to), (at_t, t_to)):
         for peer in peers:
             pl.semaphore_signal(barrier, inc=1, device_id=to(peer), device_id_type=MESH)
@@ -85,9 +85,12 @@
     ld = ld_v[...]
     at_r = lax.broadcasted_iota(jnp.int32, (GROUP, GROUP), 0)
     at_c = lax.broadcasted_iota(jnp.int32, (GROUP, GROUP), 1)
-    lower = (at_r >= at_c).astype(F32)
-    high = lax.Precision.HIGHEST
-    cum_t = lax.dot_general(lower, ld, NT, precision=high, preferred_element_type=F32)
+    lower = (at_r >= at_c).astype(BF16)
+    top = ld.astype(BF16)
+    rest = ld - top.astype(F32)
+    middle = rest.astype(BF16)
+    parts = (top, middle, (rest - middle.astype(F32)).astype(BF16))
+    cum_t = sum(lax.dot_general(lower, q, NT, preferred_element_type=F32) for q in parts)
     lane = lax.broadcasted_iota(jnp.int32, (GROUP, 128), 1)
     left = lane < HEADDIM
     for h in range(heads):
@@ -157,8 +160,7 @@
     for to in y_to:
         remote(own_row, dec_y.at[me_y], dy_send, dy_recv, at_y(to)).start()
 
-    upper = (at_r <= at_c).astype(F32)
-    row_v[...] = jnp.dot(ld, upper, precision=high, preferred_element_type=F32)
+    row_v[...] = sum(lax.dot_general(q, lower, NT, preferred_element_type=F32) for q in parts)
     gram_t = lax.dot_general(b_v[...], c_v[...], NT, preferred_element_type=F32)
     hb = GROUP // 2
     tri = (
@@ -262,19 +264,17 @@
     scan_row(FORWARD, 1)
     wait_bytes(dec_y.at[others_y], dy_recv)
     carry_row(FORWARD, 0)
-    give_back(FORWARD, 0, early)
+    give_back(FORWARD, 0, z_up)
     scan_row(BACKWARD, 0)
     carry_row(FORWARD, 1)
-    give_back(FORWARD, 1, early)
-    give_back(FORWARD, 0, late)
+    give_back(FORWARD, 1, z_up)
     scan_row(BACKWARD, 1)
     carry_row(BACKWARD, 0)
-    give_back(BACKWARD, 0, early)
-    give_back(FORWARD, 1, late)
+    give_back(BACKWARD, 0, z_up[:1])
     carry_row(BACKWARD, 1)
-    give_back(BACKWARD, 1, early)
-    give_back(BACKWARD, 0, late)
-    give_back(BACKWARD, 1, late)
+    give_back(BACKWARD, 1, z_up[:1])
+    give_back(BACKWARD, 0, z_up[1:])
+    give_back(BACKWARD, 1, z_up[1:])
 
     def collect(way):
         for part_at in range(HALVES):

time: 52.9 us -> 51.1 us (0.966)
  Pallas kernels: 52.1 us -> 50.1 us
    pallas_call x1, Pallas kernels: 51.3 us -> 49.3 us  [shards(): pl.pallas_call(functools.partial(kernel, ny, nz, nt), out_shape=out_shape...]
where the time goes in v3:
time: 51.1 us; the launch traced here: 50.7 us
  Pallas kernels  50.1 us (98%)
  between operations  0.64 us (1%)
    pallas_call x1, Pallas kernels, shards(): pl.pallas_call(functools.partial(kernel, ny, nz, nt), out_shape=out_shape...  49.3 us

profile of v3, /device:TPU:1, one launch (start us, length us, event | category | flops | bytes accessed | tf_op | source)
XLA Modules:
  0.0 50.7 jit_solution(2016297454382432289)
XLA Ops:
  0.6 49.3 %mixer_backward.1 = (bf16[256,640]{1,0:T(8,128)(2,1)S(1)}, f32[32,128]{1,0:T(8,128)S(1)}, f32[32,128]{1,0:T(8,128)S(1)}) custom-call(bf16[256,640]{1,0:T(8,128)(2,1)} %x_hbm.1, f32[10,256]{1,0:T(8,128)} %ld_hbm.1, bf16[256,128]{1,0:T(8,128)(2,1)} %b_hbm.1, bf16[256,128]{1,0:T(8,128)(2,1)} %c_hbm.1, bf16[256,640]{1,0:T(8,128)(2,1)} %g_hbm.1), custom_call_target="tpu_custom_call" | custom-call | tf_op jit(solution)/shard_map/mixer_backward/pallas_call | solution.py:351
  50.0 0.8 %write_out.1 = (bf16[256,640]{1,0:T(8,128)(2,1)}, f32[32,128]{1,0:T(8,128)}, f32[32,128]{1,0:T(8,128)}) custom-call(bf16[256,640]{1,0:T(8,128)(2,1)S(1)} %get-tuple-element.6.gx, f32[32,128]{1,0:T(8,128)S(1)} %get-tuple-element.7.gb, f32[32,128]{1,0:T(8,128)S(1)} %get-tuple-element.8.gc), custom_call_target="tpu_custom_call" | custom-call | tf_op jit(solution)/shard_map/write_out/pallas_call | solution.py:403

commit v4 on v3

--- a/solution.py
+++ b/solution.py
@@ -40,7 +40,7 @@
     own_dec, dec_z, dec_y, own_row, edge,
     states, rec_z, pre, total, rec_y, back, ret, hbf,
     acc_f, gx_acc, part, rec_t,
-    load_sem,
+    load_sem, row_in, rows_in,
     dz_send, dz_recv, dy_send, dy_recv, z_send, z_recv, y_send, y_recv, r_send, r_recv, t_send, t_recv,
 ):
     heads = ld_v.shape[0]
@@ -77,9 +77,20 @@
     z_up = [k + jnp.where(me_z <= k, 1, 0) for k in range(nz - 1)]
     y_to = [lax.rem(me_y + off, ny) for off in ring_offsets(ny)]
     t_to = [lax.rem(me_t + off, nt) for off in ring_offsets(nt)]
-    for to, peers in ((at_z, z_to), (at_y, y_to), (at_t, t_to)):
-        for peer in peers:
-            pl.semaphore_signal(barrier, inc=1, device_id=to(peer), device_id_type=MESH)
+    first = me_z == 0
+
+    def signal(sem, to):
+        pl.semaphore_signal(sem, inc=1, device_id=to, device_id_type=MESH)
+
+    for peer in z_to:
+        signal(barrier, at_z(peer))
+    for peer in t_to:
+        signal(barrier, at_t(peer))
+
+    @pl.when(first)
+    def _():
+        for peer in y_to:
+            signal(barrier, at_y(peer))
 
     loads[0].wait()
     ld = ld_v[...]
@@ -109,7 +120,13 @@
     bt = b_v[...].astype(F32).T.astype(BF16)
     states[FORWARD] = jnp.dot(bt, xw_v[...], preferred_element_type=F32)
 
-    pl.semaphore_wait(barrier, nz + ny + nt - 3)
+    pl.semaphore_wait(barrier, nz + nt - 2 + jnp.where(first, ny - 1, 0))
+
+    @pl.when(first)
+    def _():
+        for peer in y_to:
+            signal(row_in, at_y(peer))
+
 
     def remote(src, dst, send, recv, to):
         return pltpu.make_async_remote_copy(src, dst, send, recv, to, MESH)
@@ -117,23 +134,25 @@
     for to in z_to:
         remote(own_dec, dec_z.at[me_z], dz_send, dz_recv, at_z(to)).start()
 
-    def send_pieces(way):
-        for part_at in range(HALVES):
-            chunk = way * HALVES + part_at
-            for to in z_to:
-                remote(
-                    states.at[way, pl.ds(pl.multiple_of(to * piece + part_at * half, half), half)],
-                    rec_z.at[way, part_at, me_z],
-                    z_send.at[chunk],
-                    z_recv.at[chunk],
-                    at_z(to),
-                ).start()
+    def send_pieces(way, part_at):
+        chunk = way * HALVES + part_at
+        for to in z_to:
+            remote(
+                states.at[way, pl.ds(pl.multiple_of(to * piece + part_at * half, half), half)],
+                rec_z.at[way, part_at, me_z],
+                z_send.at[chunk],
+                z_recv.at[chunk],
+                at_z(to),
+            ).start()
+
+    def keep_own(way):
         for part_at in range(HALVES):
             rec_z[way, part_at, me_z] = states[
                 way, pl.ds(pl.multiple_of(me_z * piece + part_at * half, half), half)
             ]
 
-    send_pieces(FORWARD)
+    send_pieces(FORWARD, 0)
+    keep_own(FORWARD)
     dec_z[me_z] = own_dec[...]
 
     loads[3].wait()
@@ -144,7 +163,10 @@
         gw_v[:, at] = (g_v[:, at].astype(F32) * jnp.exp(cum)).astype(BF16)
     ct = c_v[...].astype(F32).T.astype(BF16)
     states[BACKWARD] = jnp.dot(ct, gw_v[...], preferred_element_type=F32)
-    send_pieces(BACKWARD)
+    send_pieces(BACKWARD, 0)
+    send_pieces(FORWARD, 1)
+    send_pieces(BACKWARD, 1)
+    keep_own(BACKWARD)
 
     others_z, others_y, others_t = pl.ds(0, nz - 1), pl.ds(0, ny - 1), pl.ds(0, nt - 1)
     wait_bytes(dec_z.at[others_z], dz_recv)
@@ -157,8 +179,6 @@
     for z in reversed(range(nz)):
         edge[BACKWARD, z] = behind
         behind = behind * dec_z[z]
-    for to in y_to:
-        remote(own_row, dec_y.at[me_y], dy_send, dy_recv, at_y(to)).start()
 
     row_v[...] = sum(lax.dot_general(q, lower, NT, preferred_element_type=F32) for q in parts)
     gram_t = lax.dot_general(b_v[...], c_v[...], NT, preferred_element_type=F32)
@@ -196,6 +216,16 @@
     part[1] = jnp.dot(first_t.astype(BF16), c_v[...], preferred_element_type=F32)
     part[0] = jnp.dot(first_t.T.astype(BF16), b_v[...], preferred_element_type=F32)
 
+    @pl.when(first)
+    def _():
+        pl.semaphore_wait(row_in, ny - 1)
+        for z in range(1, nz):
+            signal(rows_in, at_z(z))
+
+    pl.when(me_z > 0)(lambda: pl.semaphore_wait(rows_in, 1))
+    for to in y_to:
+        remote(own_row, dec_y.at[me_y], dy_send, dy_recv, at_y(to)).start()
+
     def y_copy(way, part_at, y):
         chunk = way * HALVES + part_at
         return remote(
@@ -261,20 +291,20 @@
     cut = (nz - 1) // 2
     early, late = z_up[:cut], z_up[cut:]
     scan_row(FORWARD, 0)
-    scan_row(FORWARD, 1)
+    scan_row(BACKWARD, 0)
     wait_bytes(dec_y.at[others_y], dy_recv)
     carry_row(FORWARD, 0)
     give_back(FORWARD, 0, z_up)
-    scan_row(BACKWARD, 0)
+    scan_row(FORWARD, 1)
+    carry_row(BACKWARD, 0)
+    give_back(BACKWARD, 0, z_up)
+    scan_row(BACKWARD, 1)
     carry_row(FORWARD, 1)
-    give_back(FORWARD, 1, z_up)
-    scan_row(BACKWARD, 1)
-    carry_row(BACKWARD, 0)
-    give_back(BACKWARD, 0, z_up[:1])
+    give_back(FORWARD, 1, z_up[:2])
     carry_row(BACKWARD, 1)
-    give_back(BACKWARD, 1, z_up[:1])
-    give_back(BACKWARD, 0, z_up[1:])
-    give_back(BACKWARD, 1, z_up[1:])
+    give_back(BACKWARD, 1, z_up[:2])
+    give_back(FORWARD, 1, z_up[2:])
+    give_back(BACKWARD, 1, z_up[2:])
 
     def collect(way):
         for part_at in range(HALVES):
@@ -382,6 +412,8 @@
             vmem((2, GROUP, STATE), F32),
             vmem((2, nt, rows, STATE), F32),
             dma((5,)),
+            pltpu.SemaphoreType.REGULAR,
+            pltpu.SemaphoreType.REGULAR,
             dma,
             dma,
             dma,

time: 51.1 us -> 49.8 us (0.975)
  Pallas kernels: 50.1 us -> 49 us
    pallas_call x1, Pallas kernels: 49.3 us -> 48.2 us  [shards(): pl.pallas_call(functools.partial(kernel, ny, nz, nt), out_shape=out_shape...]
where the time goes in v4:
time: 49.8 us; the launch traced here: 49.6 us
  Pallas kernels  49 us (98%)
  between operations  0.64 us (1%)
    pallas_call x1, Pallas kernels, shards(): pl.pallas_call(functools.partial(kernel, ny, nz, nt), out_shape=out_shape...  48.2 us

profile of v4, /device:TPU:1, one launch (start us, length us, event | category | flops | bytes accessed | tf_op | source)
XLA Modules:
  0.0 49.6 jit_solution(6974913109958820941)
XLA Ops:
  0.6 48.2 %mixer_backward.1 = (bf16[256,640]{1,0:T(8,128)(2,1)S(1)}, f32[32,128]{1,0:T(8,128)S(1)}, f32[32,128]{1,0:T(8,128)S(1)}) custom-call(bf16[256,640]{1,0:T(8,128)(2,1)} %x_hbm.1, f32[10,256]{1,0:T(8,128)} %ld_hbm.1, bf16[256,128]{1,0:T(8,128)(2,1)} %b_hbm.1, bf16[256,128]{1,0:T(8,128)(2,1)} %c_hbm.1, bf16[256,640]{1,0:T(8,128)(2,1)} %g_hbm.1), custom_call_target="tpu_custom_call" | custom-call | tf_op jit(solution)/shard_map/mixer_backward/pallas_call | solution.py:381
  48.9 0.8 %write_out.1 = (bf16[256,640]{1,0:T(8,128)(2,1)}, f32[32,128]{1,0:T(8,128)}, f32[32,128]{1,0:T(8,128)}) custom-call(bf16[256,640]{1,0:T(8,128)(2,1)S(1)} %get-tuple-element.6.gx, f32[32,128]{1,0:T(8,128)S(1)} %get-tuple-element.7.gb, f32[32,128]{1,0:T(8,128)S(1)} %get-tuple-element.8.gc), custom_call_target="tpu_custom_call" | custom-call | tf_op jit(solution)/shard_map/write_out/pallas_call | solution.py:435

commit v5 on v4

--- a/solution.py
+++ b/solution.py
@@ -247,14 +247,9 @@
         )
 
     def y_targets(way, fn):
-        def body(y, carry):
-            fn(y)
-            return carry
-
-        if way == FORWARD:
-            lax.fori_loop(me_y + 1, ny, body, 0)
-        else:
-            lax.fori_loop(0, me_y, body, 0)
+        for off in reversed(range(1, ny)):
+            y = me_y + off if way == FORWARD else me_y - off
+            pl.when((y < ny) & (y >= 0))(functools.partial(fn, y))
 
     def scan_row(way, part_at):
         wait_bytes(rec_z.at[way, part_at, others_z], z_recv.at[way * HALVES + part_at])

time: 49.8 us -> 49.4 us (level)
  no operation moved by 1% of the time
where the time goes in v5:
time: 49.4 us; the launch traced here: 49.2 us
  Pallas kernels  48.6 us (98%)
  between operations  0.64 us (1%)
    pallas_call x1, Pallas kernels, shards(): pl.pallas_call(functools.partial(kernel, ny, nz, nt), out_shape=out_shape...  47.8 us

profile of v5, /device:TPU:1, one launch (start us, length us, event | category | flops | bytes accessed | tf_op | source)
XLA Modules:
  0.0 49.2 jit_solution(5989388871158916970)
XLA Ops:
  0.6 47.8 %mixer_backward.1 = (bf16[256,640]{1,0:T(8,128)(2,1)S(1)}, f32[32,128]{1,0:T(8,128)S(1)}, f32[32,128]{1,0:T(8,128)S(1)}) custom-call(bf16[256,640]{1,0:T(8,128)(2,1)} %x_hbm.1, f32[10,256]{1,0:T(8,128)} %ld_hbm.1, bf16[256,128]{1,0:T(8,128)(2,1)} %b_hbm.1, bf16[256,128]{1,0:T(8,128)(2,1)} %c_hbm.1, bf16[256,640]{1,0:T(8,128)(2,1)} %g_hbm.1), custom_call_target="tpu_custom_call" | custom-call | tf_op jit(solution)/shard_map/mixer_backward/pallas_call | solution.py:376
  48.5 0.8 %write_out.1 = (bf16[256,640]{1,0:T(8,128)(2,1)}, f32[32,128]{1,0:T(8,128)}, f32[32,128]{1,0:T(8,128)}) custom-call(bf16[256,640]{1,0:T(8,128)(2,1)S(1)} %get-tuple-element.6.gx, f32[32,128]{1,0:T(8,128)S(1)} %get-tuple-element.7.gb, f32[32,128]{1,0:T(8,128)S(1)} %get-tuple-element.8.gc), custom_call_target="tpu_custom_call" | custom-call | tf_op jit(solution)/shard_map/write_out/pallas_call | solution.py:430
